TPU v7x, 32 devices: a whole 2x2x4 slice. The times are simulated.
32 devices in a mesh: dp: 16 (over z, y, core), tensor: 2 (over x).
Axes of the slice: x: 2, y: 2, z: 4, core: 2. Of those that a mesh axis runs over, the one named last changes fastest.
Arguments:
- tokens: bfloat16 [4096, 1024], P(('dp', 'tensor')), may hold values from -24 to 24, as said below
- segment_ids: int32 [16, 256], P('dp'), may hold values from 0 to 3, never falling along the last dimension, each value on 1 to 128 neighbouring positions
- norm1_gain: float32 [1024], replicated, may hold values from 0.5 to 1.5
- in_proj: bfloat16 [1024, 3, 1024], P('dp', None, 'tensor'), may hold values from -0.1875 to 0.1875
- conv_weight: float32 [3, 1024], replicated, may hold values from -3 to 3
- out_proj: bfloat16 [1024, 1024], P('dp', 'tensor'), may hold values from -0.1875 to 0.1875
- norm2_gain: float32 [1024], replicated, may hold values from 0.5 to 1.5
- gate_up: bfloat16 [1024, 2, 4608], P('dp', None, 'tensor'), may hold values from -0.1875 to 0.1875
- down_proj: bfloat16 [1024, 4608], P('dp', 'tensor'), may hold values from -0.1875 to 0.1875
- cotangent: bfloat16 [4096, 1024], P(('dp', 'tensor')), may hold values from -6 to 6
Outputs:
- block_out: float32 [4096, 1024], P(('dp', 'tensor'))
- grad_tokens: float32 [4096, 1024], P(('dp', 'tensor'))
- grad_norm1: float32 [1024], replicated
- grad_in_proj: float32 [1024, 3, 1024], P('dp', None, 'tensor')
- grad_conv: float32 [3, 1024], replicated
- grad_out_proj: float32 [1024, 1024], P('dp', 'tensor')
- grad_norm2: float32 [1024], replicated
- grad_gate_up: float32 [1024, 2, 4608], P('dp', None, 'tensor')
- grad_down: float32 [1024, 4608], P('dp', 'tensor')
Inputs may be any that keep to these rules, and one draw needn't show every extreme that they name: `segment_ids`: along each row the document numbers never fall; each document spans 1 to 128 tokens and one spans exactly 128. `tokens`: real values.
All inputs are finite; a program needn't handle non-finite values.
Results may differ from a plain program's by a relative error of at most 0.009.
Values may be sent and summed in bfloat16 or wider, within the bound.
A program may use at most 128 MiB of HBM per device.

v0:
```python
import functools

import jax
import jax.numpy as jnp
from jax import lax
from jax.experimental import pallas as pl
from jax.experimental.pallas import tpu as pltpu
from jax.sharding import PartitionSpec as P

EPSILON = 1e-05


def rms_forward(values, norm_gain):
    factor = lax.rsqrt(jnp.mean(values * values, axis=-1, keepdims=True) + EPSILON)
    return (values * factor * norm_gain, factor)


def rms_backward(values, factor, norm_gain, upstream):
    scaled = upstream * norm_gain
    result = factor * scaled - values * (factor * factor * factor) * jnp.mean(
        scaled * values, axis=-1, keepdims=True
    )
    return (result, jnp.sum(upstream * values * factor, axis=0))


MESH = pl.DeviceIdType.MESH

WAYS = (-1, -1, 1, 1, -1)
BACKWARD = (1, 0, 1, 0, 0)


def chip_at(pos, chips):
    back = pos // (chips // 2)
    return (1 - back) * 2 * pos + back * (2 * (chips - 1 - pos) + 1)


def ring_place(chips):
    me = lax.axis_index("dp")
    core, chip = me % 2, me // 2
    odd = chip % 2
    pos = (1 - odd) * (chip // 2) + odd * (chips - 1 - chip // 2)

    def owner(steps):
        return chip_at((pos + steps + 2 * chips) % chips, chips)

    return me, core, chip, owner


def greet(others):
    barrier = pltpu.get_barrier_semaphore()
    peer = 1 - lax.axis_index("tensor")
    pl.semaphore_signal(barrier, inc=1, device_id={"tensor": peer}, device_id_type=MESH)
    for other in others:
        pl.semaphore_signal(barrier, inc=1, device_id={"dp": other}, device_id_type=MESH)
    pl.semaphore_wait(barrier, len(others) + 1)


def across(source, into, send_sem, recv_sem):
    return pltpu.make_async_remote_copy(
        src_ref=source,
        dst_ref=into,
        send_sem=send_sem,
        recv_sem=recv_sem,
        device_id={"tensor": 1 - lax.axis_index("tensor")},
        device_id_type=MESH,
    )


def gather_kernel(chips, ways, *refs):
    count = len(ways)
    pairs = (len(refs) - 2 * count - 7) // 2
    swaps_in, refs = refs[:pairs], refs[pairs:]
    ins, refs = refs[:count], refs[count:]
    swaps_out, refs = refs[:pairs], refs[pairs:]
    outs = refs[:count]
    own_sem, send_sem, recv_sem, hand_sem, take_sem, out_sem, in_sem = refs[count:]
    me, core, chip, owner = ring_place(chips)
    partner = chip * 2 + 1 - core
    nexts = {way: owner(way) * 2 + core for way in (1, -1)}
    greet((nexts[1], nexts[-1], partner))
    own, started = [], []
    for i in range(pairs):
        swap = across(swaps_in[i], swaps_out[i], out_sem.at[i], in_sem.at[i])
        swap.start()
        started.append((swap, True))
    arriving, direct = [None] * count, {}
    for step in range(chips):
        for i, way in enumerate(ways):
            slot = owner(-way * step) * 2 + core
            if step:
                arriving[i].wait_recv()
            source = outs[i].at[slot] if step else ins[i]
            if step < chips - 1 and not (BACKWARD[i] and step == chips - 2):
                ring = pltpu.make_async_remote_copy(
                    src_ref=source,
                    dst_ref=outs[i].at[slot],
                    send_sem=send_sem.at[i, step],
                    recv_sem=recv_sem.at[i, step],
                    device_id={"dp": nexts[way]},
                    device_id_type=MESH,
                )
                ring.start()
                arriving[i] = ring
                started.append((ring, False))
            if BACKWARD[i] and step == chips - 2:
                arriving[i] = direct[i]
            if BACKWARD[i] and step == 0:
                direct[i] = pltpu.make_async_remote_copy(
                    src_ref=source,
                    dst_ref=outs[i].at[slot],
                    send_sem=send_sem.at[i, chips - 2],
                    recv_sem=recv_sem.at[i, chips - 2],
                    device_id={"dp": nexts[-way]},
                    device_id_type=MESH,
                )
                direct[i].start()
                started.append((direct[i], False))
            hand = pltpu.make_async_remote_copy(
                src_ref=source,
                dst_ref=outs[i].at[slot],
                send_sem=hand_sem.at[i, step],
                recv_sem=take_sem.at[i, step],
                device_id={"dp": partner},
                device_id_type=MESH,
            )
            hand.start()
            started.append((hand, True))
            if step == 0:
                keep = pltpu.make_async_copy(ins[i], outs[i].at[me], own_sem.at[i])
                keep.start()
                own.append(keep)
    for copy, handed in started:
        copy.wait_send()
        if handed:
            copy.wait_recv()
    for keep in own:
        keep.wait()


def gather_all(swapped, shards, ways, ranks):
    chips, count, pairs = ranks // 2, len(shards), len(swapped)
    dma = pltpu.SemaphoreType.DMA
    outs = pl.pallas_call(
        functools.partial(gather_kernel, chips, ways),
        out_shape=[jax.ShapeDtypeStruct(s.shape, s.dtype) for s in swapped]
        + [jax.ShapeDtypeStruct((ranks,) + s.shape, s.dtype) for s in shards],
        in_specs=[pl.BlockSpec(memory_space=pltpu.VMEM)] * (pairs + count),
        out_specs=[pl.BlockSpec(memory_space=pltpu.VMEM)] * pairs
        + [pl.BlockSpec(memory_space=pl.ANY)] * count,
        scratch_shapes=[
            dma((count,)),
            dma((count, chips - 1)),
            dma((count, chips - 1)),
            dma((count, chips)),
            dma((count, chips)),
            dma((pairs,)),
            dma((pairs,)),
        ],
        compiler_params=pltpu.CompilerParams(collective_id=1, has_side_effects=True),
    )(*swapped, *shards)
    full = [g.reshape(ranks * s.shape[0], s.shape[1]) for g, s in zip(outs[pairs:], shards)]
    return outs[:pairs], full


def scatter_kernel(chips, ways, *refs):
    count = len(ways)
    small_in, row_in, refs = refs[0], refs[1], refs[2:]
    ins, refs = refs[:count], refs[count:]
    small_out, row_out, refs = refs[0], refs[1], refs[2:]
    outs, refs = refs[:count], refs[count:]
    mine = refs[:count]
    theirs = refs[count : 2 * count]
    moving = refs[2 * count : 3 * count]
    smalls, folded, folded_other, refs = *refs[3 * count : 3 * count + 3], refs[3 * count + 3 :]
    load_sem, send_sem, recv_sem, hand_sem, take_sem, own_sem, out_sem, in_sem = refs[:8]
    small_send, small_recv, small_hand, small_take = refs[8:]
    me, core, chip, owner = ring_place(chips)
    partner = chip * 2 + 1 - core
    nexts = {way: owner(way) * 2 + core for way in (1, -1)}
    greet((nexts[1], nexts[-1], partner))
    row_swap = across(row_in, row_out, out_sem.at[0], in_sem.at[0])
    row_swap.start()
    keep = pltpu.make_async_copy(small_in, smalls.at[me], own_sem)
    keep.start()
    small_hops, small_hands = [], []
    loads, swaps = {}, {}
    for step in range(chips):
        for i, way in enumerate(ways):
            target = owner(-way * (step + 1))
            load = pltpu.make_async_copy(
                ins[i].at[target * 2 + core], mine[i].at[step], load_sem.at[i, step]
            )
            load.start()
            loads[i, step] = load
            swap = pltpu.make_async_remote_copy(
                src_ref=ins[i].at[target * 2 + 1 - core],
                dst_ref=theirs[i].at[step],
                send_sem=hand_sem.at[i, step],
                recv_sem=take_sem.at[i, step],
                device_id={"dp": partner},
                device_id_type=MESH,
            )
            swap.start()
            swaps[i, step] = swap
    hops = {}
    for step in range(chips):
        slot = owner(-step) * 2 + core
        if step:
            small_hops[step - 1].wait_recv()
        source = smalls.at[slot] if step else small_in
        if step < chips - 1:
            ring = pltpu.make_async_remote_copy(
                src_ref=source,
                dst_ref=smalls.at[slot],
                send_sem=small_send.at[step],
                recv_sem=small_recv.at[step],
                device_id={"dp": nexts[1]},
                device_id_type=MESH,
            )
            ring.start()
            small_hops.append(ring)
        hand = pltpu.make_async_remote_copy(
            src_ref=source,
            dst_ref=smalls.at[slot],
            send_sem=small_hand.at[step],
            recv_sem=small_take.at[step],
            device_id={"dp": partner},
            device_id_type=MESH,
        )
        hand.start()
        small_hands.append(hand)
        if step == chips - 1:
            keep.wait()
            for hand in small_hands:
                hand.wait_recv()
            folded[...] = lax.fori_loop(
                1, 2 * chips, lambda k, total: total + smalls[k], smalls[0]
            )
            fold_swap = across(folded, folded_other, out_sem.at[1], in_sem.at[1])
            fold_swap.start()
        for i, way in enumerate(ways):
            rows = ins[i].shape[1]
            tile = min(rows, 16)
            loads[i, step].wait()
            swaps[i, step].wait_recv()
            last = step == chips - 1
            added = [step - 1] if step > BACKWARD[i] else []
            if last and BACKWARD[i]:
                added.append(0)
            for hop in added:
                hops[i, hop].wait_recv()
            into = outs[i] if last else (moving[i].at[step - 1] if added else mine[i].at[step])

            @pl.loop(0, rows // tile)
            def _(block):
                span = pl.ds(pl.multiple_of(block * tile, tile), tile)
                total = mine[i][step, span, :].astype(jnp.float32) + theirs[i][
                    step, span, :
                ].astype(jnp.float32)
                for hop in added:
                    total = total + moving[i][hop, span, :].astype(jnp.float32)
                into[span, :] = total.astype(into.dtype)

            if not last:
                hop = pltpu.make_async_remote_copy(
                    src_ref=into,
                    dst_ref=moving[i].at[step],
                    send_sem=send_sem.at[i, step],
                    recv_sem=recv_sem.at[i, step],
                    device_id={"dp": nexts[-way if BACKWARD[i] and step == 0 else way]},
                    device_id_type=MESH,
                )
                hop.start()
                hops[i, step] = hop
    fold_swap.wait()
    small_out[...] = folded[...] + folded_other[...]
    row_swap.wait()
    for copy in list(hops.values()) + list(swaps.values()) + small_hops + small_hands:
        copy.wait_send()


def scatter_all(small, rows, grads, ways, ranks):
    chips, count = ranks // 2, len(grads)
    grads = [g.reshape(ranks, g.shape[0] // ranks, g.shape[1]) for g in grads]
    dma = pltpu.SemaphoreType.DMA
    blocks = [g.shape[1:] for g in grads]
    return pl.pallas_call(
        functools.partial(scatter_kernel, chips, ways),
        out_shape=[jax.ShapeDtypeStruct(v.shape, v.dtype) for v in (small, rows)]
        + [jax.ShapeDtypeStruct(b, jnp.float32) for b in blocks],
        in_specs=[pl.BlockSpec(memory_space=pltpu.VMEM)] * 2
        + [pl.BlockSpec(memory_space=pl.ANY)] * count,
        out_specs=[pl.BlockSpec(memory_space=pltpu.VMEM)] * (count + 2),
        scratch_shapes=[pltpu.VMEM((chips,) + b, jnp.bfloat16) for b in blocks]
        + [pltpu.VMEM((chips,) + b, jnp.bfloat16) for b in blocks]
        + [pltpu.VMEM((chips - 1,) + b, jnp.bfloat16) for b in blocks]
        + [pltpu.VMEM((ranks,) + small.shape, small.dtype)]
        + [pltpu.VMEM(small.shape, small.dtype)] * 2
        + [
            dma((count, chips)),
            dma((count, chips - 1)),
            dma((count, chips - 1)),
            dma((count, chips)),
            dma((count, chips)),
            dma,
            dma((2,)),
            dma((2,)),
            dma((chips - 1,)),
            dma((chips - 1,)),
            dma((chips,)),
            dma((chips,)),
        ],
        compiler_params=pltpu.CompilerParams(
            collective_id=2, has_side_effects=True, vmem_limit_bytes=56 * 1024 * 1024
        ),
    )(small, rows, *grads)


def both(values):
    other = lax.ppermute(values, "tensor", [(0, 1), (1, 0)])
    return jnp.concatenate([values, other], axis=0)


def halves_sum(terms):
    half = terms.shape[0] // 2
    sent = lax.ppermute(terms[half:].astype(jnp.bfloat16), "tensor", [(0, 1), (1, 0)])
    return terms[:half] + sent.astype(jnp.float32)


def reset_masks(segment):
    padded = jnp.concatenate([jnp.full((2,), -1, segment.dtype), segment])
    same_one, same_two = segment == padded[1:-1], segment == padded[:-2]
    masks = jnp.stack([same_one, same_two]).astype(jnp.float32)
    half = segment.shape[0] // 2
    turned = jnp.concatenate([masks[:, half:], masks[:, :half]], axis=1)
    masks = jnp.where(lax.axis_index("tensor") == 0, masks, turned)
    return (masks[0][:, None], masks[1][:, None])


def turn(values, offset):
    return jnp.concatenate([values[-offset:], values[:-offset]], axis=0)


def dot(left, right, dims):
    return lax.dot_general(left, right, (dims, ((), ())), preferred_element_type=jnp.float32)


def local(
    tokens,
    segment_ids,
    norm1_gain,
    in_proj,
    conv_weight,
    out_proj,
    norm2_gain,
    gate_up,
    down_proj,
    cotangent,
    *,
    ranks,
):
    rows, _, channels = in_proj.shape
    inputs = tokens.astype(jnp.float32)
    normed_one, factor_one = rms_forward(inputs, norm1_gain)
    normed_one = normed_one.astype(jnp.bfloat16)
    (normed_other, cot_other), (in_full, out_full, gate_full, up_full, down_full) = gather_all(
        [normed_one, cotangent],
        [
            in_proj.reshape(rows, 3 * channels),
            out_proj,
            gate_up[:, 0, :],
            gate_up[:, 1, :],
            down_proj,
        ],
        WAYS,
        ranks,
    )
    rows_one = jnp.concatenate([normed_one, normed_other], axis=0)
    cot_rows = jnp.concatenate([cotangent, cot_other], axis=0)
    offset = lax.axis_index("tensor") * channels
    kernel = lax.dynamic_slice_in_dim(conv_weight, offset, channels, 1)
    mask_one, mask_two = reset_masks(segment_ids[0])
    projected = dot(rows_one, in_full, ((1,), (0,)))
    b_part = projected[:, :channels]
    c_part = projected[:, channels : 2 * channels]
    x_part = projected[:, 2 * channels :]
    mixed_in = b_part * x_part
    mixed_one = mask_one * turn(mixed_in, 1)
    mixed_two = mask_two * turn(mixed_in, 2)
    conv_out = kernel[0] * mixed_in + kernel[1] * mixed_one + kernel[2] * mixed_two
    gated = (c_part * conv_out).astype(jnp.bfloat16)
    resid = inputs + halves_sum(dot(gated, out_full, ((1,), (1,))))
    normed_two, factor_two = rms_forward(resid, norm2_gain)
    rows_two = both(normed_two.astype(jnp.bfloat16))
    gate_lin = dot(rows_two, gate_full, ((1,), (0,)))
    up_lin = dot(rows_two, up_full, ((1,), (0,)))
    sigmoid_gate = jax.nn.sigmoid(gate_lin)
    activ = gate_lin * sigmoid_gate
    hidden = (activ * up_lin).astype(jnp.bfloat16)
    ffn_terms = dot(hidden, down_full, ((1,), (1,)))
    grad_down = dot(cot_rows, hidden, ((0,), (0,))).astype(jnp.bfloat16)
    back_hidden = dot(cot_rows, down_full, ((1,), (0,)))
    back_gate = (
        back_hidden * up_lin * sigmoid_gate * (1.0 + gate_lin * (1.0 - sigmoid_gate))
    ).astype(jnp.bfloat16)
    back_up = (back_hidden * activ).astype(jnp.bfloat16)
    grad_gate = dot(rows_two, back_gate, ((0,), (0,))).astype(jnp.bfloat16)
    grad_up = dot(rows_two, back_up, ((0,), (0,))).astype(jnp.bfloat16)
    back_normed2 = halves_sum(
        dot(back_gate, gate_full, ((1,), (1,))) + dot(back_up, up_full, ((1,), (1,)))
    )
    resid_part, gain_two = rms_backward(resid, factor_two, norm2_gain, back_normed2)
    back_resid = cotangent.astype(jnp.float32) + resid_part
    resid_rows = both(back_resid.astype(jnp.bfloat16))
    grad_out = dot(resid_rows, gated, ((0,), (0,))).astype(jnp.bfloat16)
    back_gated = dot(resid_rows, out_full, ((1,), (0,)))
    back_c = back_gated * conv_out
    back_conv = back_gated * c_part
    back_mixed = (
        kernel[0] * back_conv
        + turn(kernel[1] * mask_one * back_conv, -1)
        + turn(kernel[2] * mask_two * back_conv, -2)
    )
    conv_local = jnp.stack(
        [
            jnp.sum(back_conv * mixed_in, axis=0),
            jnp.sum(back_conv * mixed_one, axis=0),
            jnp.sum(back_conv * mixed_two, axis=0),
        ]
    )
    back_proj = jnp.concatenate(
        [back_mixed * x_part, back_c, back_mixed * b_part], axis=1
    ).astype(jnp.bfloat16)
    grad_in = dot(rows_one, back_proj, ((0,), (0,))).astype(jnp.bfloat16)
    back_normed1 = halves_sum(dot(back_proj, in_full, ((1,), (1,))))
    input_part, gain_one = rms_backward(inputs, factor_one, norm1_gain, back_normed1)
    grad_tokens = back_resid + input_part
    conv_placed = lax.dynamic_update_slice_in_dim(
        jnp.zeros(conv_weight.shape, jnp.float32), conv_local, offset, 1
    )
    small = jnp.concatenate(
        [gain_one[None], gain_two[None], conv_placed, jnp.zeros_like(conv_placed)], axis=0
    )
    half = ffn_terms.shape[0] // 2
    small, ffn_other, in_shard, out_shard, gate_shard, up_shard, down_shard = scatter_all(
        small,
        ffn_terms[half:].astype(jnp.bfloat16),
        [grad_in, grad_out, grad_gate, grad_up, grad_down],
        WAYS,
        ranks,
    )
    block_out = resid + (ffn_terms[:half] + ffn_other.astype(jnp.float32))
    return (
        block_out,
        grad_tokens,
        small[0],
        in_shard.reshape(in_proj.shape),
        small[2:5],
        out_shard,
        small[1],
        jnp.stack([gate_shard, up_shard], axis=1),
        down_shard,
    )


def solution(mesh):
    placed = (
        P(("dp", "tensor"), None),
        P("dp", None),
        P(),
        P("dp", None, "tensor"),
        P(),
        P("dp", "tensor"),
        P(),
        P("dp", None, "tensor"),
        P("dp", "tensor"),
        P(("dp", "tensor"), None),
    )
    return jax.shard_map(
        functools.partial(local, ranks=mesh.shape["dp"]),
        mesh=mesh,
        in_specs=placed,
        out_specs=(
            P(("dp", "tensor"), None),
            P(("dp", "tensor"), None),
            P(),
            P("dp", None, "tensor"),
            P(),
            P("dp", "tensor"),
            P(),
            P("dp", None, "tensor"),
            P("dp", "tensor"),
        ),
        check_vma=False,
    )
```

profile of v0, /device:TPU:0, one launch (start us, length us, event | category | flops | bytes accessed | tf_op | source)
XLA Modules:
  0.0 279.4 jit_solution(1548013588298196619)
XLA Ops:
  0.7 1.1 fusion.1
  1.8 1.6 copy.32
  3.4 2.3 fusion.26
  5.8 0.8 fusion.3.refs_0_
  6.6 0.9 copy_bitcast_fusion.1
  7.5 98.8 %shard_map.169 = (bf16[128,1024]{1,0:T(8,128)(2,1)}, bf16[128,1024]{1,0:T(8,128)(2,1)}, bf16[16,64,1536]{2,1,0:T(8,128)(2,1)}, bf16[16,64,512]{2,1,0:T(8,128)(2,...) custom-call(bf16[128,1024]{1,0:T(8,128)(2,1)} %fusion.3.refs_0_, ...), custom_call_target="tpu_custom_call" | custom-call | tf_op jit(solution)/shard_map/pallas_call | solution.py:143
  106.3 3.0 %fusion.13 = f32[256,1536]{1,0:T(8,128)S(1)} fusion(bf16[1024,1536]{1,0:T(8,128)(2,1)} %bitcast.67, bf16[128,1024]{1,0:T(8,128)(2,1)} %get-tuple-element.23, bf16[128,1024]{1,0:T(8,128)(2,1)S(1)} %copy-done.3), kind=kOutput, calls=%fused_computation.63 | convolution fusion | flops 806354944 | bytes 5242880 | tf_op jit(solution)/shard_map/dot_general | solution.py:345
  109.6 0.9 constant_dynamic-slice_fusion
  110.5 0.3 multiply_convert_fusion.7
  110.8 0.5 fusion.30
  111.3 1.6 collective-permute-start
  112.9 7.0 %collective-permute-done = bf16[128,1024]{1,0:T(8,128)(2,1)S(1)} collective-permute-done((bf16[128,1024]{1,0:T(8,128)(2,1)S(1)}, bf16[128,1024]{1,0:T(8,128)(2,1)S(1)}, u32[]{:S(2)}, u32[]{:S(2)}) %collective-permute-start) | collective-permute-done | bytes 262176 | tf_op jit(solution)/shard_map/ppermute | solution.py:326
  120.3 1.6 collective-permute-start.1
  121.9 1.4 fusion.32
  123.2 4.8 %collective-permute-done.1 = bf16[128,1024]{1,0:T(8,128)(2,1)S(1)} collective-permute-done((bf16[128,1024]{1,0:T(8,128)(2,1)S(1)}, bf16[128,1024]{1,0:T(8,128)(2,1)S(1)}, u32[]{:S(2)}, u32[]{:S(2)}) %collective-permute-start.1) | collective-permute-done | bytes 262176 | tf_op jit(solution)/shard_map/ppermute | solution.py:320
  128.1 1.4 fusion.22
  129.5 2.1 multiply_convert_fusion
  131.6 1.4 fusion.31
  133.0 3.7 %convolution_convert_fusion = bf16[1024,2304]{1,0:T(8,128)(2,1)} fusion(bf16[256,1024]{1,0:T(8,128)(2,1)S(1)} %constant_dynamic-update-slice_fusion, bf16[256,2304]{1,0:T(8,128)(2,1)S(1)} %get-tuple-element.74), kind=kOutput, calls=%fused_computation | convolution fusion | flops 1210318848 | bytes 6422528 | tf_op jit(solution)/shard_map/dot_general | solution.py:345
  136.7 1.6 fusion.33
  138.3 1.4 convolution_add_fusion
  139.7 1.6 collective-permute-start.2
  141.3 0.7 slice.198.refs_1_
  142.0 3.6 %convolution_convert_fusion.2 = bf16[1024,2304]{1,0:T(8,128)(2,1)} fusion(bf16[256,2304]{1,0:T(8,128)(2,1)S(1)} %get-tuple-element.73, bf16[128,1024]{1,0:T(8,128)(2,1)S(1)} %collective-permute-done.1, bf16[128,1024]{1,0:T(8,128)(2,1)S(1)} %multiply_convert_fusion.6), kind=kOutput, calls=%fused_computation.2 | convolution fusion | flops 1211367424 | bytes 6422528 | tf_op jit(solution)/shard_map/dot_general | solution.py:345
  145.6 1.1 collective-permute-done.2
  147.1 1.6 collective-permute-start.3
  148.6 3.6 %convolution_convert_fusion.1 = bf16[1024,2304]{1,0:T(8,128)(2,1)} fusion(bf16[256,2304]{1,0:T(8,128)(2,1)S(1)} %get-tuple-element.72, bf16[128,1024]{1,0:T(8,128)(2,1)S(1)} %collective-permute-done.1, bf16[128,1024]{1,0:T(8,128)(2,1)S(1)} %multiply_convert_fusion.6), kind=kOutput, calls=%fused_computation.1 | convolution fusion | flops 1211367424 | bytes 6422528 | tf_op jit(solution)/shard_map/dot_general | solution.py:345
  152.3 1.3 collective-permute-done.3
  153.5 0.5 multiply_multiply_fusion
  154.1 0.3 multiply_reduce_fusion.2
  154.4 0.3 multiply_convert_fusion.5
  154.8 1.5 copy-done.2
  156.3 1.0 fusion.14
  157.4 2.7 convolution_convert_fusion.3
  160.1 1.6 collective-permute-start.4
  161.6 1.5 convolution_convert_fusion.4
  163.1 3.4 %collective-permute-done.4 = bf16[128,1024]{1,0:T(8,128)(2,1)S(1)} collective-permute-done((bf16[128,1024]{1,0:T(8,128)(2,1)S(1)}, bf16[128,1024]{1,0:T(8,128)(2,1)S(1)}, u32[]{:S(2)}, u32[]{:S(2)}) %collective-permute-start.4) | collective-permute-done | bytes 262176 | tf_op jit(solution)/shard_map/ppermute | solution.py:326
  166.5 0.2 fusion.9
  166.7 0.6 pad_maximum_fusion.11.refs_0_
  167.3 101.1 %shard_map.170 = (f32[8,1024]{1,0:T(8,128)}, bf16[128,1024]{1,0:T(8,128)(2,1)}, f32[64,1536]{1,0:T(8,128)}, f32[64,512]{1,0:T(8,128)}, f32[64,2304]{1,0:T(8,128)...) custom-call(f32[8,1024]{1,0:T(8,128)} %pad_maximum_fusion.11.refs_0_, bf16[128,1024]{1,0:T(8,128)(2,1)} %slice.198.refs_1_, ...), custom_call_target="tpu_custom_call" | custom-call | tf_op jit(solution)/shard_map/pallas_call | solution.py:287
  268.4 1.5 fusion.27
  269.9 1.4 slice.137
  271.3 1.8 fusion.10
  273.1 1.8 copy.36
  275.0 1.9 copy.28
  276.9 1.0 fusion.8
  278.0 0.7 copy.41
  278.6 0.8 copy.42
  (77 shorter events, 1.5 us)
Async XLA Ops:
  0.6 5.1 %copy-start = (bf16[128,1024]{1,0:T(8,128)(2,1)S(1)}, bf16[128,1024]{1,0:T(8,128)(2,1)}, u32[]{:S(2)}) copy-start(bf16[128,1024]{1,0:T(8,128)(2,1)} %param.10) | copy-start | bytes 786436
  0.7 5.1 %copy-start.15 = (f32[1024]{0:T(1024)S(1)}, f32[1024]{0:T(1024)}, u32[]{:S(2)}) copy-start(f32[1024]{0:T(1024)} %param.12) | copy-start | bytes 12292
  6.6 99.6 %copy-start.3 = (bf16[128,1024]{1,0:T(8,128)(2,1)S(1)}, bf16[128,1024]{1,0:T(8,128)(2,1)}, u32[]{:S(2)}) copy-start(bf16[128,1024]{1,0:T(8,128)(2,1)} %fusion.3.refs_0_) | copy-start | bytes 786436
  106.3 3.1 %copy-start.16 = (s32[1,256]{1,0:T(1,128)S(1)}, s32[1,256]{1,0:T(1,128)}, u32[]{:S(2)}) copy-start(s32[1,256]{1,0:T(1,128)} %param.11) | copy-start | bytes 3076
  109.3 1.5 copy-start.1
  110.5 2.4 copy-start.5
  110.8 2.1 copy-start.12
  110.8 9.4 %copy-start.14 = (f32[1024]{0:T(1024)S(1)}, f32[1024]{0:T(1024)}, u32[]{:S(2)}) copy-start(f32[1024]{0:T(1024)} %param.16) | copy-start | bytes 12292
  110.8 11.1 %copy-start.17 = (bf16[16,64,2304]{2,1,0:T(8,128)(2,1)S(1)}, bf16[16,64,2304]{2,1,0:T(8,128)(2,1)}, u32[]{:S(2)}) copy-start(bf16[16,64,2304]{2,1,0:T(8,128)(2,1)} %get-tuple-element.28) | copy-start | bytes 14155780
  111.3 8.6 %collective-permute-start = (bf16[128,1024]{1,0:T(8,128)(2,1)S(1)}, bf16[128,1024]{1,0:T(8,128)(2,1)S(1)}, u32[]{:S(2)}, u32[]{:S(2)}) collective-permute-start(bf16[128,1024]{1,0:T(8,128)(2,1)S(1)} %slice.201), channel_id=1, source_target_pairs={{0,1},{1,0},{2,3},{3,2},{4,5},{5,4},{6,7},{7,6},{8,9},{9,8},{10,11... | collective-permute-start | bytes 786440 | tf_op jit(solution)/shard_map/ppermute | solution.py:326
  120.2 7.9 %slice-start = ((s8[4718592]{0:T(1024)(128)(4,1)}), s8[4194304]{0:T(1024)(128)(4,1)S(1)}, s32[]{:S(2)}) async-start(s8[4718592]{0:T(1024)(128)(4,1)} %bitcast.95), calls=%async_computation | async-start | bytes 8388608
  120.2 9.3 %slice-start.2 = ((s8[4718592]{0:T(1024)(128)(4,1)}), s8[4194304]{0:T(1024)(128)(4,1)S(1)}, s32[]{:S(2)}) async-start(s8[4718592]{0:T(1024)(128)(4,1)} %bitcast.99), calls=%async_computation.2 | async-start | bytes 8388608
  120.3 7.8 %collective-permute-start.1 = (bf16[128,1024]{1,0:T(8,128)(2,1)S(1)}, bf16[128,1024]{1,0:T(8,128)(2,1)S(1)}, u32[]{:S(2)}, u32[]{:S(2)}) collective-permute-start(bf16[128,1024]{1,0:T(8,128)(2,1)S(1)} %multiply_convert_fusion.6), channel_id=1, source_target_pairs={{0,1},{1,0},{2,3},{3,2},{4,5},{5,4},{6,7},{7,6},{8,9},{9,8},{10,11... | collective-permute-start | bytes 786440 | tf_op jit(solution)/shard_map/ppermute | solution.py:320
  121.9 6.2 %slice-start.1 = ((s8[4718592]{0:T(1024)(128)(4,1)}), s8[524288]{0:T(1024)(128)(4,1)S(1)}, s32[]{:S(2)}) async-start(s8[4718592]{0:T(1024)(128)(4,1)} %bitcast.95), calls=%async_computation.1 | async-start | bytes 1048576
  121.9 7.6 %slice-start.3 = ((s8[4718592]{0:T(1024)(128)(4,1)}), s8[524288]{0:T(1024)(128)(4,1)S(1)}, s32[]{:S(2)}) async-start(s8[4718592]{0:T(1024)(128)(4,1)} %bitcast.99), calls=%async_computation.3 | async-start | bytes 1048576
  133.0 8.3 %copy-start.6 = (f32[256,1024]{1,0:T(8,128)}, f32[256,1024]{1,0:T(8,128)S(1)}, u32[]{:S(2)}) copy-start(f32[256,1024]{1,0:T(8,128)S(1)} %fusion.31) | copy-start | bytes 3145732
  139.7 6.9 %collective-permute-start.2 = (bf16[128,1024]{1,0:T(8,128)(2,1)S(1)}, bf16[128,1024]{1,0:T(8,128)(2,1)S(1)}, u32[]{:S(2)}, u32[]{:S(2)}) collective-permute-start(bf16[128,1024]{1,0:T(8,128)(2,1)S(1)} %slice.200), channel_id=1, source_target_pairs={{0,1},{1,0},{2,3},{3,2},{4,5},{5,4},{6,7},{7,6},{8,9},{9,8},{10,11... | collective-permute-start | bytes 786440 | tf_op jit(solution)/shard_map/ppermute | solution.py:326
  147.1 6.4 %collective-permute-start.3 = (bf16[128,1024]{1,0:T(8,128)(2,1)S(1)}, bf16[128,1024]{1,0:T(8,128)(2,1)S(1)}, u32[]{:S(2)}, u32[]{:S(2)}) collective-permute-start(bf16[128,1024]{1,0:T(8,128)(2,1)S(1)} %get-tuple-element.66), channel_id=1, source_target_pairs={{0,1},{1,0},{2,3},{3,2},{4,5},{5,4},{6,7},{7,6},{8,9},{9,8},{10,11... | collective-permute-start | bytes 786440 | tf_op jit(solution)/shard_map/ppermute | solution.py:320
  154.4 1.9 copy-start.2
  156.3 1.0 copy-start.4
  156.3 1.0 copy-start.11
  160.1 6.4 %collective-permute-start.4 = (bf16[128,1024]{1,0:T(8,128)(2,1)S(1)}, bf16[128,1024]{1,0:T(8,128)(2,1)S(1)}, u32[]{:S(2)}, u32[]{:S(2)}) collective-permute-start(bf16[128,1024]{1,0:T(8,128)(2,1)S(1)} %slice.199), channel_id=1, source_target_pairs={{0,1},{1,0},{2,3},{3,2},{4,5},{5,4},{6,7},{7,6},{8,9},{9,8},{10,11... | collective-permute-start | bytes 786440 | tf_op jit(solution)/shard_map/ppermute | solution.py:326
  167.3 103.9 %copy-start.7 = (f32[256,1024]{1,0:T(8,128)S(1)}, f32[256,1024]{1,0:T(8,128)}, u32[]{:S(2)}) copy-start(f32[256,1024]{1,0:T(8,128)} %copy-done.6) | copy-start | bytes 3145732
  268.4 6.5 %copy-start.9 = (f32[64,2304]{1,0:T(8,128)S(1)}, f32[64,2304]{1,0:T(8,128)}, u32[]{:S(2)}) copy-start(f32[64,2304]{1,0:T(8,128)} %get-tuple-element.34) | copy-start | bytes 1769476
  268.4 6.5 %copy-start.10 = (f32[64,2304]{1,0:T(8,128)S(1)}, f32[64,2304]{1,0:T(8,128)}, u32[]{:S(2)}) copy-start(f32[64,2304]{1,0:T(8,128)} %get-tuple-element.35) | copy-start | bytes 1769476
  275.0 3.0 %copy-start.13 = (f32[64,512]{1,0:T(8,128)S(1)}, f32[64,512]{1,0:T(8,128)}, u32[]{:S(2)}) copy-start(f32[64,512]{1,0:T(8,128)} %get-tuple-element.110) | copy-start | bytes 393220
  275.0 3.6 %copy-start.8 = (f32[64,2304]{1,0:T(8,128)S(1)}, f32[64,2304]{1,0:T(8,128)}, u32[]{:S(2)}) copy-start(f32[64,2304]{1,0:T(8,128)} %get-tuple-element.113) | copy-start | bytes 1769476
where the time goes:
time: 280 us; the launch traced here: 279 us
  Pallas kernels  200 us (71%)
  matrix products  29.1 us (10%)
  waiting for transfers between devices  17.6 us (6%)
  local copies, waits for them, and re-layouts  16.3 us (6%)
  starting transfers between devices  7.79 us (3%)
  other arithmetic  7.64 us (3%)
    pallas_call x1, Pallas kernels, scatter_all(): pl.pallas_call(functools.partial(scatter_kernel, chips, ways), out_shape=...  101 us
    pallas_call x1, Pallas kernels, gather_all(): pl.pallas_call(functools.partial(gather_kernel, chips, ways), out_shape=[...  98.8 us
    dot_general x15, matrix products, dot(): lax.dot_general(left, right, (dims, ((), ())), preferred_element_type=jnp...  29.1 us
    ppermute x3, waiting for transfers between devices, halves_sum(): lax.ppermute(terms[half:].astype(jnp.bfloat16), 'tensor', [(0, 1), (1, 0)])  11.5 us
    ppermute x2, waiting for transfers between devices, both(): other = lax.ppermute(values, 'tensor', [(0, 1), (1, 0)])  6.1 us
  transfers between devices with their start and end apart: 5, of which 5 were waited for; matrix products, arithmetic and copies ran while one was open for 4% of the time, Pallas kernels for 0%

commit v1 on v0

v1 whole, which is shorter than its diff:
```python
import functools
from types import SimpleNamespace

import jax
import jax.numpy as jnp
from jax import lax
from jax.experimental import pallas as pl
from jax.experimental.pallas import tpu as pltpu
from jax.sharding import PartitionSpec as P

EPSILON = 1e-05
MESH = pl.DeviceIdType.MESH
F32, BF16 = jnp.float32, jnp.bfloat16
NN, NT = ((1,), (0,)), ((1,), (1,))


def chip_at(pos, chips):
    back = pos // (chips // 2)
    return (1 - back) * 2 * pos + back * (2 * (chips - 1 - pos) + 1)


def ring_place(chips):
    me = lax.axis_index("dp")
    core, chip = me % 2, me // 2
    odd = chip % 2
    pos = (1 - odd) * (chip // 2) + odd * (chips - 1 - chip // 2)

    def owner(steps):
        return chip_at((pos + steps + 2 * chips) % chips, chips)

    return me, core, chip, owner


def greet(others):
    barrier = pltpu.get_barrier_semaphore()
    peer = 1 - lax.axis_index("tensor")
    pl.semaphore_signal(barrier, inc=1, device_id={"tensor": peer}, device_id_type=MESH)
    for other in others:
        pl.semaphore_signal(barrier, inc=1, device_id={"dp": other}, device_id_type=MESH)
    pl.semaphore_wait(barrier, len(others) + 1)


def mm(left, right, dims):
    return lax.dot_general(left, right, (dims, ((), ())), preferred_element_type=F32)


def flat(block):
    count, rows, cols = block.shape
    if rows % 16:
        return block.astype(F32).reshape(count * rows, cols).astype(BF16)
    return block.reshape(count * rows, cols)


def tile_of(cols):
    return next(t for t in (768, 512, 256) if cols % t == 0)


def span(index, size):
    return pl.ds(pl.multiple_of(index * size, size), size)


def pieces(cols, count):
    tiles = cols // 128
    sizes = [(tiles * (i + 1) // count - tiles * i // count) * 128 for i in range(count)]
    return [(sum(sizes[:i]), sizes[i]) for i in range(count)]


def block_kernel(dims, names, *refs):
    chips, ranks, rows, depth, channels, hidden_units, half = dims
    r = SimpleNamespace(**dict(zip(names, refs)))
    me, core, chip, owner = ring_place(chips)
    partner = chip * 2 + 1 - core
    nexts = {way: owner(way) * 2 + core for way in (1, -1)}
    column = lax.axis_index("tensor") * channels
    per_block = 256 // rows
    blocks = depth // 256
    small_tile = 256
    last = chips - 1
    if not hasattr(r, "s_send"):
        r.s_send, r.s_recv, r.s_hand, r.s_take = r.g_send, r.g_recv, r.g_hand, r.g_take

    def remote(src, dst, send, recv, where):
        return pltpu.make_async_remote_copy(
            src_ref=src,
            dst_ref=dst,
            send_sem=send,
            recv_sem=recv,
            device_id=where,
            device_id_type=MESH,
        )

    gathers = []
    for j, way in ((0, 1), (1, 1), (2, -1)):
        gathers.append((0, way, r.in_sh.at[j], lambda slot, j=j: r.in_full.at[j, slot]))
    gathers.append((0, -1, r.out_sh, lambda slot: r.out_full.at[slot]))
    for way, shard, full in ((1, r.gate_sh, r.gate_full), (-1, r.up_sh, r.up_full)):
        for start, size in pieces(hidden_units, 2):
            cols = pl.ds(start, size)
            gathers.append(
                (1, way, shard.at[:, cols], lambda slot, full=full, cols=cols: full.at[slot, :, cols])
            )
    for k, (start, size) in enumerate(pieces(hidden_units, 4)):
        cols = pl.ds(start, size)
        gathers.append(
            (2, 1 - 2 * (k // 2), r.down_sh.at[:, cols], lambda slot, cols=cols: r.down_full.at[slot, :, cols])
        )
    arriving, unsent, taken, kept = {}, {0: [], 1: [], 2: []}, {0: [], 1: [], 2: []}, {0: [], 1: [], 2: []}

    def gather(group, step):
        for f, (own_group, way, shard, place) in enumerate(gathers):
            if own_group != group:
                continue
            slot = owner(-way * step) * 2 + core
            if step:
                arriving[f].wait_recv()
            source = place(slot) if step else shard
            if step < last:
                ring = remote(
                    source, place(slot), r.g_send.at[f, step], r.g_recv.at[f, step], {"dp": nexts[way]}
                )
                ring.start()
                arriving[f] = ring
                unsent[group].append(ring)
            hand = remote(
                source, place(slot), r.g_hand.at[f, step], r.g_take.at[f, step], {"dp": partner}
            )
            hand.start()
            taken[group].append(hand)
            unsent[group].append(hand)
            if step == 0:
                keep = pltpu.make_async_copy(shard, place(me), r.g_own.at[f])
                keep.start()
                kept[group].append(keep)

    def gathered(group):
        for hand in taken[group]:
            hand.wait_recv()
        for keep in kept[group]:
            keep.wait()

    def sent(group):
        for copy in unsent[group]:
            copy.wait_send()

    def across(index, source, into):
        copy = remote(
            source,
            into,
            r.x_send.at[index],
            r.x_recv.at[index],
            {"tensor": 1 - lax.axis_index("tensor")},
        )
        copy.start()
        return copy

    scatters = []
    for k, (start, size) in enumerate(pieces(hidden_units, 4)):
        way = 1 - 2 * (k // 2)
        scatters.append((0, way, r.grad_down, r.theirs_down, r.moving_down, start, size, r.slope, 0, start))
    for way, grad, theirs, moving, place in (
        (1, r.down_full, r.theirs_gate, r.moving_gate, 1),
        (-1, r.gate_full, r.theirs_up, r.moving_up, 2),
    ):
        for start, size in pieces(hidden_units, 2):
            scatters.append((1, way, grad, theirs, moving, start, size, r.slope, place * rows, start))
    for j, way in ((0, 1), (1, 1), (2, -1), (3, -1)):
        scatters.append(
            (2, way, r.up_full, r.theirs_io, r.moving_io, j * channels, channels, r.activ, j * rows, 0)
        )
    swaps, hops = {}, {}

    def swap(group):
        for step in range(chips):
            for f, (own_group, way, grad, theirs, _, start, size, *_) in enumerate(scatters):
                if own_group != group:
                    continue
                target = owner(-way * (step + 1))
                cols = pl.ds(start, size)
                copy = remote(
                    grad.at[target * 2 + 1 - core, :, cols],
                    theirs.at[step, :, cols],
                    r.s_hand.at[f, step],
                    r.s_take.at[f, step],
                    {"dp": partner},
                )
                copy.start()
                swaps[f, step] = copy

    def scatter(group, step):
        tile = min(rows, 16)
        for f, (own_group, way, grad, theirs, moving, start, size, stage, row, col) in enumerate(scatters):
            if own_group != group:
                continue
            slot = owner(-way * (step + 1)) * 2 + core
            cols = pl.ds(start, size)
            swaps[f, step].wait_recv()
            if step:
                hops[f, step - 1].wait_recv()

            @pl.loop(0, rows // tile)
            def _(block):
                at = span(block, tile)
                total = grad[slot, at, cols].astype(F32) + theirs[step, at, cols].astype(F32)
                if step:
                    total = total + moving[step - 1, at, cols].astype(F32)
                if step == last:
                    stage[pl.ds(pl.multiple_of(row + block * tile, tile), tile), pl.ds(col, size)] = total
                elif step:
                    moving[step - 1, at, cols] = total.astype(BF16)
                else:
                    grad[slot, at, cols] = total.astype(BF16)

            if step < last:
                source = moving.at[step - 1, :, cols] if step else grad.at[slot, :, cols]
                hop = remote(
                    source, moving.at[step, :, cols], r.s_send.at[f, step], r.s_recv.at[f, step], {"dp": nexts[way]}
                )
                hop.start()
                hops[f, step] = hop

    saves = []

    def save(index, source, into):
        copy = pltpu.make_async_copy(source, into, r.o_sem.at[index])
        copy.start()
        saves.append(copy)

    def row_loop(body):
        @pl.loop(0, half // 16)
        def _(index):
            body(span(index, 16))

    def turned(source, into):
        @pl.loop(0, depth // 128)
        def _(index):
            at = span(index, 128)
            into[at, :] = source[:, at].astype(F32).T.astype(BF16)

    def outer(left, right, into, offset, low, high):
        cols = right.shape[1]
        tile = tile_of(cols)

        @pl.loop(low, high)
        def _(block):
            @pl.loop(0, cols // tile)
            def _(n):
                value = mm(left[span(block, 256), :], right[:, span(n, tile)], NN)
                at = pl.ds(pl.multiple_of(offset + n * tile, 128), tile)
                into[span(block, per_block), :, at] = value.reshape(per_block, rows, tile).astype(BF16)

    def factor_of(values):
        return lax.rsqrt(jnp.mean(values * values, axis=-1, keepdims=True) + EPSILON)

    def norm_one(at):
        values = r.tokens[at, :].astype(F32)
        r.rows_one[at, :] = (values * factor_of(values) * r.gain1[...]).astype(BF16)
        r.cot_rows[at, :] = r.cot[at, :]

    def project():
        @pl.loop(0, 3)
        def _(j):
            @pl.loop(0, channels // small_tile)
            def _(n):
                cols = span(n, small_tile)
                r.projected[j, :, cols] = mm(r.rows_one[...], flat(r.in_full[j, :, :, cols]), NN)

    def shifted(values):
        return pltpu.roll(values, 1, 0), pltpu.roll(values, 2, 0)

    def taps(n):
        at = pl.ds(pl.multiple_of(column + n * 128, 128), 128)
        return [r.conv[k : k + 1, at] for k in range(3)], at

    def convolve():
        @pl.loop(0, channels // 128)
        def _(n):
            cols = span(n, 128)
            kernel, _ = taps(n)
            mixed = r.projected[0, :, cols] * r.projected[2, :, cols]
            one, two = shifted(mixed)
            out = kernel[0] * mixed + kernel[1] * (r.masks[0] * one) + kernel[2] * (r.masks[1] * two)
            r.conv_out[:, cols] = out
            r.gated[:, cols] = (r.projected[1, :, cols] * out).astype(BF16)

    def out_terms():
        @pl.loop(0, blocks)
        def _(b):
            value = mm(r.gated[...], flat(r.out_full[span(b, per_block), :, :]), NT)
            at = span(b, 256)
            r.acc[:, at] = value[:half]
            r.away0[:, at] = value[half:].astype(BF16)

    def residual(at):
        values = r.tokens[at, :].astype(F32) + (r.acc[at, :] + r.near0[at, :].astype(F32))
        r.resid[at, :] = values
        r.rows_two[at, :] = (values * factor_of(values) * r.gain2[...]).astype(BF16)

    def gate_up(low, high):
        @pl.loop(low, high)
        def _(n):
            cols = span(n, small_tile)
            gate = mm(r.rows_two[...], flat(r.gate_full[:, :, cols]), NN)
            up = mm(r.rows_two[...], flat(r.up_full[:, :, cols]), NN)
            sigmoid = jax.nn.sigmoid(gate)
            activ = gate * sigmoid
            r.hidden[:, cols] = (activ * up).astype(BF16)
            r.activ[:, cols] = activ
            r.slope[:, cols] = up * sigmoid * (1.0 + gate * (1.0 - sigmoid))

    def back_hidden(low, high):
        @pl.loop(low, high)
        def _(n):
            cols = span(n, small_tile)
            back = mm(r.cot_rows[...], flat(r.down_full[:, :, cols]), NN)
            r.back_gate[:, cols] = (back * r.slope[:, cols]).astype(BF16)
            r.back_up[:, cols] = (back * r.activ[:, cols]).astype(BF16)

    def ffn_terms():
        @pl.loop(0, blocks)
        def _(b):
            value = mm(r.hidden[...], flat(r.down_full[span(b, per_block), :, :]), NT)
            at = span(b, 256)
            r.block_out[:, at] = r.resid[:, at] + value[:half]
            r.away1[:, at] = value[half:].astype(BF16)

    def back_two(low, high):
        @pl.loop(low, high)
        def _(b):
            rows_at = span(b, per_block)
            value = mm(r.back_gate[...], flat(r.gate_full[rows_at, :, :]), NT)
            value = value + mm(r.back_up[...], flat(r.up_full[rows_at, :, :]), NT)
            at = span(b, 256)
            r.acc[:, at] = value[:half]
            r.away2[:, at] = value[half:].astype(BF16)

    def norm_back(values, gain, upstream, small_row):
        factor = factor_of(values)
        scaled = upstream * gain
        mean = jnp.mean(scaled * values, axis=-1, keepdims=True)
        r.small[small_row : small_row + 1, :] += jnp.sum(upstream * values * factor, axis=0, keepdims=True)
        return factor * scaled - values * (factor * factor * factor) * mean

    def residual_back(at):
        upstream = r.acc[at, :] + r.near2[at, :].astype(F32)
        back = r.cot[at, :].astype(F32) + norm_back(r.resid[at, :], r.gain2[...], upstream, 1)
        r.grad_tokens[at, :] = back
        r.resid_rows[at, :] = back.astype(BF16)

    def mixer_back():
        @pl.loop(0, channels // 128)
        def _(n):
            cols = span(n, 128)
            kernel, at = taps(n)
            gated_back = mm(r.resid_rows[...], flat(r.out_full[:, :, cols]), NN)
            b_part, c_part, x_part = [r.projected[j, :, cols] for j in range(3)]
            mixed = b_part * x_part
            one, two = shifted(mixed)
            one, two = r.masks[0] * one, r.masks[1] * two
            conv_back = gated_back * c_part
            mixed_back = (
                kernel[0] * conv_back
                + pltpu.roll(kernel[1] * (r.masks[0] * conv_back), 2 * half - 1, 0)
                + pltpu.roll(kernel[2] * (r.masks[1] * conv_back), 2 * half - 2, 0)
            )
            for k, term in enumerate((mixed, one, two)):
                r.small[2 + k : 3 + k, at] = jnp.sum(conv_back * term, axis=0, keepdims=True)
            r.back_proj[0, :, cols] = (mixed_back * x_part).astype(BF16)
            r.back_proj[1, :, cols] = (gated_back * r.conv_out[:, cols]).astype(BF16)
            r.back_proj[2, :, cols] = (mixed_back * b_part).astype(BF16)

    def back_one():
        @pl.loop(0, blocks)
        def _(b):
            rows_at = span(b, per_block)
            value = mm(r.back_proj[0], flat(r.in_full[0, rows_at, :, :]), NT)
            for j in (1, 2):
                value = value + mm(r.back_proj[j], flat(r.in_full[j, rows_at, :, :]), NT)
            at = span(b, 256)
            r.acc[:, at] = value[:half]
            r.away3[:, at] = value[half:].astype(BF16)

    def tokens_back(at):
        upstream = r.acc[at, :] + r.near3[at, :].astype(F32)
        r.grad_tokens[at, :] += norm_back(r.tokens[at, :].astype(F32), r.gain1[...], upstream, 0)

    small_hops = []

    def small_hop(step):
        slot = owner(-step)
        if step:
            small_hops[step - 1].wait_recv()
        if step < last:
            hop = remote(
                r.smalls.at[slot], r.smalls.at[slot], r.m_send.at[step], r.m_recv.at[step], {"dp": nexts[1]}
            )
            hop.start()
            small_hops.append(hop)

    first, second = pl.ds(0, half), pl.ds(half, half)

    greet((nexts[1], nexts[-1], partner))
    gather(0, 0)
    cot_swap = across(0, r.cot, r.cot_rows.at[second])
    row_loop(norm_one)
    rows_swap = across(1, r.rows_one.at[first], r.rows_one.at[second])
    r.small[...] = jnp.zeros_like(r.small)
    for step in range(1, last):
        gather(0, step)
    gather(1, 0)
    gather(0, last)
    gathered(0)
    rows_swap.wait_recv()
    project()
    convolve()
    out_terms()
    terms_swap = across(2, r.away0, r.near0)
    gather(1, 1)
    cot_swap.wait_recv()
    turned(r.cot_rows, r.across_t)
    mid = max(3, last // 2)
    for step in range(2, mid):
        gather(1, step)
    terms_swap.wait_recv()
    row_loop(residual)
    two_swap = across(3, r.rows_two.at[first], r.rows_two.at[second])
    for step in range(mid, last):
        gather(1, step)
    gather(2, 0)
    gather(1, last)
    gathered(1)
    two_swap.wait_recv()
    tiles = hidden_units // small_tile
    cuts = [tiles * k // 3 for k in range(4)]
    at_step = 1
    for k in range(3):
        gate_up(cuts[k], cuts[k + 1])
        gather(2, at_step)
        at_step += 1
    bounds = [blocks * k // 2 for k in range(3)]
    outer(r.across_t, r.hidden, r.grad_down, 0, bounds[0], bounds[1])
    gather(2, at_step)
    outer(r.across_t, r.hidden, r.grad_down, 0, bounds[1], bounds[2])
    swap(0)
    for step in range(at_step + 1, last):
        gather(2, step)
    turned(r.rows_two, r.across_t)
    scatter(0, 0)
    gather(2, last)
    gathered(2)
    back_hidden(0, tiles)
    scatter(0, 1)
    ffn_terms()
    ffn_swap = across(4, r.away1, r.near1)
    back_two(0, blocks // 2)
    scatter(0, 2)
    back_two(blocks // 2, blocks)
    back_swap = across(5, r.away2, r.near2)
    sent(2)
    outer(r.across_t, r.back_gate, r.down_full, 0, bounds[0], bounds[1])
    scatter(0, 3)
    outer(r.across_t, r.back_gate, r.down_full, 0, bounds[1], bounds[2])
    sent(1)
    outer(r.across_t, r.back_up, r.gate_full, 0, bounds[0], bounds[1])
    scatter(0, 4)
    outer(r.across_t, r.back_up, r.gate_full, 0, bounds[1], bounds[2])
    swap(1)
    back_swap.wait_recv()
    row_loop(residual_back)
    resid_swap = across(6, r.resid_rows.at[first], r.resid_rows.at[second])
    for step in range(5, last):
        scatter(0, step)
    scatter(1, 0)
    scatter(0, last)
    resid_swap.wait_recv()
    mixer_back()
    scatter(1, 1)
    back_one()
    last_swap = across(7, r.away3, r.near3)
    turned(r.rows_one, r.across_t)
    for j in range(3):
        outer(r.across_t, r.back_proj.at[j], r.up_full, j * channels, 0, blocks)
    scatter(1, 2)
    turned(r.resid_rows, r.across_t)
    outer(r.across_t, r.gated, r.up_full, 3 * channels, 0, blocks)
    swap(2)
    scatter(1, 3)
    last_swap.wait_recv()
    row_loop(tokens_back)
    pair = remote(r.small, r.small_pair, r.m_pair.at[0], r.m_pair.at[1], {"dp": partner})
    pair.start()
    ffn_swap.wait_recv()

    @row_loop
    def _(at):
        r.block_out[at, :] += r.near1[at, :].astype(F32)

    for step in range(4, last):
        scatter(1, step)
    scatter(2, 0)
    pair.wait_recv()
    r.smalls[chip] = r.small[...] + r.small_pair[...]
    small_hop(0)
    scatter(1, last)
    for step in range(1, last):
        small_hop(step)
        scatter(2, step)
    small_hop(last)
    r.folded[...] = lax.fori_loop(1, chips, lambda k, total: total + r.smalls[k], r.smalls[0])
    fold_swap = across(8, r.folded, r.folded_other)
    save(0, r.slope.at[pl.ds(0, rows), :], r.o_down)
    save(1, r.slope.at[pl.ds(rows, rows), :], r.o_gate)
    save(2, r.slope.at[pl.ds(2 * rows, rows), :], r.o_up)
    scatter(2, last)
    for j in range(3):
        save(3 + j, r.activ.at[pl.ds(j * rows, rows), pl.ds(0, channels)], r.o_in.at[j])
    save(6, r.activ.at[pl.ds(3 * rows, rows), pl.ds(0, channels)], r.o_out)
    fold_swap.wait_recv()
    r.o_small[...] = r.folded[...] + r.folded_other[...]
    for copy in saves:
        copy.wait()
    sent(0)
    for copy in list(hops.values()) + list(swaps.values()) + small_hops + [pair]:
        copy.wait_send()
    for copy in (
        cot_swap, rows_swap, terms_swap, two_swap, ffn_swap, back_swap, resid_swap, last_swap, fold_swap
    ):
        copy.wait_send()


def run_block(tokens, cot, masks, conv, gain1, gain2, in_sh, out_sh, gate_sh, up_sh, down_sh, ranks):
    chips = ranks // 2
    half, depth = tokens.shape
    rows, channels = out_sh.shape
    units = down_sh.shape[1]
    full = 2 * half
    vmem, dma = pltpu.VMEM, pltpu.SemaphoreType.DMA
    inputs = dict(
        tokens=tokens, cot=cot, masks=masks, conv=conv, gain1=gain1, gain2=gain2,
        in_sh=in_sh, out_sh=out_sh, gate_sh=gate_sh, up_sh=up_sh, down_sh=down_sh,
    )
    outputs = dict(
        block_out=(half, depth),
        grad_tokens=(half, depth),
        o_small=(8, depth),
        o_in=(3, rows, channels),
        o_out=(rows, channels),
        o_gate=(rows, units),
        o_up=(rows, units),
        o_down=(rows, units),
    )
    io = 3 * channels + channels
    flows = 12
    scratch = dict(
        in_full=vmem((3, ranks, rows, channels), BF16),
        out_full=vmem((ranks, rows, channels), BF16),
        gate_full=vmem((ranks, rows, units), BF16),
        up_full=vmem((ranks, rows, units), BF16),
        down_full=vmem((ranks, rows, units), BF16),
        grad_down=vmem((ranks, rows, units), BF16),
        theirs_down=vmem((chips, rows, units), BF16),
        theirs_gate=vmem((chips, rows, units), BF16),
        theirs_up=vmem((chips, rows, units), BF16),
        theirs_io=vmem((chips, rows, io), BF16),
        moving_down=vmem((chips - 1, rows, units), BF16),
        moving_gate=vmem((chips - 1, rows, units), BF16),
        moving_up=vmem((chips - 1, rows, units), BF16),
        moving_io=vmem((chips - 1, rows, io), BF16),
        rows_one=vmem((full, depth), BF16),
        cot_rows=vmem((full, depth), BF16),
        rows_two=vmem((full, depth), BF16),
        resid_rows=vmem((full, depth), BF16),
        across_t=vmem((depth, full), BF16),
        projected=vmem((3, full, channels), F32),
        conv_out=vmem((full, channels), F32),
        gated=vmem((full, channels), BF16),
        acc=vmem((half, depth), F32),
        resid=vmem((half, depth), F32),
        hidden=vmem((full, units), BF16),
        activ=vmem((full, units), F32),
        slope=vmem((full, units), F32),
        back_gate=vmem((full, units), BF16),
        back_up=vmem((full, units), BF16),
        back_proj=vmem((3, full, channels), BF16),
        small=vmem((8, depth), F32),
        small_pair=vmem((8, depth), F32),
        smalls=vmem((chips, 8, depth), F32),
        folded=vmem((8, depth), F32),
        folded_other=vmem((8, depth), F32),
        **{f"away{k}": vmem((half, depth), BF16) for k in range(4)},
        **{f"near{k}": vmem((half, depth), BF16) for k in range(4)},
        **{f"g_{k}": dma((flows, chips)) for k in ("send", "recv", "hand", "take")},
        **{f"s_{k}": dma((flows, chips)) for k in ("send", "recv", "hand", "take") if chips <= 16},
        g_own=dma((flows,)),
        x_send=dma((9,)),
        x_recv=dma((9,)),
        m_send=dma((chips - 1,)),
        m_recv=dma((chips - 1,)),
        m_pair=dma((2,)),
        o_sem=dma((7,)),
    )
    here = {"in_sh", "out_sh", "gate_sh", "up_sh", "down_sh", "o_in", "o_out", "o_gate", "o_up", "o_down"}

    def spec(name):
        return pl.BlockSpec(memory_space=pl.ANY if name in here else pltpu.VMEM)

    names = tuple(inputs) + tuple(outputs) + tuple(scratch)
    dims = (chips, ranks, rows, depth, channels, units, half)
    return pl.pallas_call(
        functools.partial(block_kernel, dims, names),
        out_shape=[jax.ShapeDtypeStruct(shape, F32) for shape in outputs.values()],
        in_specs=[spec(name) for name in inputs],
        out_specs=[spec(name) for name in outputs],
        scratch_shapes=list(scratch.values()),
        compiler_params=pltpu.CompilerParams(
            collective_id=1, has_side_effects=True, vmem_limit_bytes=67043328
        ),
    )(*inputs.values())


def reset_masks(segment):
    padded = jnp.concatenate([jnp.full((2,), -1, segment.dtype), segment])
    same_one, same_two = segment == padded[1:-1], segment == padded[:-2]
    masks = jnp.stack([same_one, same_two]).astype(F32)
    half = segment.shape[0] // 2
    turned = jnp.concatenate([masks[:, half:], masks[:, :half]], axis=1)
    masks = jnp.where(lax.axis_index("tensor") == 0, masks, turned)
    return jnp.broadcast_to(masks[:, :, None], masks.shape + (128,))


def local(
    tokens,
    segment_ids,
    norm1_gain,
    in_proj,
    conv_weight,
    out_proj,
    norm2_gain,
    gate_up,
    down_proj,
    cotangent,
    *,
    ranks,
):
    block_out, grad_tokens, small, grad_in, grad_out, grad_gate, grad_up, grad_down = run_block(
        tokens,
        cotangent,
        reset_masks(segment_ids[0]),
        conv_weight,
        norm1_gain[None],
        norm2_gain[None],
        in_proj.transpose(1, 0, 2),
        out_proj,
        gate_up[:, 0, :],
        gate_up[:, 1, :],
        down_proj,
        ranks,
    )
    return (
        block_out,
        grad_tokens,
        small[0],
        grad_in.transpose(1, 0, 2),
        small[2:5],
        grad_out,
        small[1],
        jnp.stack([grad_gate, grad_up], axis=1),
        grad_down,
    )


def solution(mesh):
    placed = (
        P(("dp", "tensor"), None),
        P("dp", None),
        P(),
        P("dp", None, "tensor"),
        P(),
        P("dp", "tensor"),
        P(),
        P("dp", None, "tensor"),
        P("dp", "tensor"),
        P(("dp", "tensor"), None),
    )
    return jax.shard_map(
        functools.partial(local, ranks=mesh.shape["dp"]),
        mesh=mesh,
        in_specs=placed,
        out_specs=(
            P(("dp", "tensor"), None),
            P(("dp", "tensor"), None),
            P(),
            P("dp", None, "tensor"),
            P(),
            P("dp", "tensor"),
            P(),
            P("dp", None, "tensor"),
            P("dp", "tensor"),
        ),
        check_vma=False,
    )
```

time: 280 us -> 241 us (0.86)
  matrix products: 29.1 us -> 0 us
  Pallas kernels: 200 us -> 225 us
  waiting for transfers between devices: 17.6 us -> 0 us
  starting transfers between devices: 7.79 us -> 0 us
  other arithmetic: 7.64 us -> 2.21 us
  local copies, waits for them, and re-layouts: 16.3 us -> 12.5 us
    dot_general x15 -> x0, matrix products: 29.1 us -> none  [dot(): lax.dot_general(left, right, (dims, ((), ())), preferred_element_type=jnp...]
    pallas_call x2 -> x1, Pallas kernels: 200 us -> 225 us  [run_block(): pl.pallas_call(functools.partial(block_kernel, dims, names), out_shape=[j...]
    ppermute x5 -> x0, waiting for transfers between devices: 17.6 us -> none  [the longest x3 11.5 us: halves_sum(): lax.ppermute(terms[half:].astype(jnp.bfloat16), 'tensor', [(0, 1), (1, 0)])]
    ppermute x5 -> x0, starting transfers between devices: 7.79 us -> none  [the longest x3 4.67 us: halves_sum(): lax.ppermute(terms[half:].astype(jnp.bfloat16), 'tensor', [(0, 1), (1, 0)])]
    reshape x2 -> x0, local copies, waits for them, and re-layouts: 3.39 us -> none  [the longest x1 1.77 us: local(): in_shard.reshape(in_proj.shape)]
    add x2 -> x0, other arithmetic: 2.87 us -> none  [the longest x1 1.85 us: local(): block_out = resid + (ffn_terms[:half] + ffn_other.astype(jnp.float32))]
    unnamed x48 -> x16, local copies, waits for them, and re-layouts: 5.03 us -> 5.75 us
  transfers between devices with their start and end apart: 5 -> 0, of which waited for: 5 -> 0; matrix products, arithmetic and copies ran while one was open for 4% -> 0% of each run, Pallas kernels for 0% -> 0%
where the time goes in v1:
time: 241 us; the launch traced here: 240 us
  Pallas kernels  225 us (93%)
  local copies, waits for them, and re-layouts  12.5 us (5%)
    pallas_call x1, Pallas kernels, run_block(): pl.pallas_call(functools.partial(block_kernel, dims, names), out_shape=[j...  225 us
    unnamed x16, local copies, waits for them, and re-layouts  5.75 us

profile of v1, /device:TPU:0, one launch (start us, length us, event | category | flops | bytes accessed | tf_op | source)
XLA Modules:
  0.0 240.3 jit_solution(9504040488810370402)
XLA Ops:
  0.6 0.9 fusion
  1.6 0.8 broadcast_in_dim.12.refs_2_
  2.4 2.3 fusion.2
  4.7 0.9 copy_bitcast_fusion
  5.6 224.8 %shard_map.169 = (f32[128,1024]{1,0:T(8,128)}, f32[128,1024]{1,0:T(8,128)}, f32[8,1024]{1,0:T(8,128)}, f32[3,64,512]{2,1,0:T(8,128)}, f32[64,512]{1,0:T(8,128)},...) custom-call(bf16[128,1024]{1,0:T(8,128)(2,1)} %refs_0_.1, bf16[128,1024]{1,0:T(8,128)(2,1)} %refs_1_.1, ...), custom_call_target="tpu_custom_call" | custom-call | tf_op jit(solution)/shard_map/pallas_call | solution.py:608
  230.4 1.4 fusion.3
  231.8 1.4 slice.34
  233.2 1.3 pad_maximum_fusion
  234.5 0.0 copy-start.2
  234.5 0.0 copy-start.1
  234.5 1.9 copy.21
  236.4 0.0 copy-done.2
  236.4 0.0 copy-start.3
  236.4 0.0 copy-start.4
  236.4 0.8 copy.31
  237.2 0.0 copy-done.1
  237.2 0.0 copy-start
  237.2 0.8 copy.32
  238.0 0.0 copy-done.3
  238.0 0.7 copy.33
  238.8 0.0 copy-done.4
  238.8 0.7 copy.34
  239.4 0.0 copy-done
  239.4 0.8 copy.35
  (5 shorter events, 0.0 us)
Async XLA Ops:
  234.5 1.9 copy-start.2
  234.5 2.7 %copy-start.1 = (f32[128,1024]{1,0:T(8,128)S(1)}, f32[128,1024]{1,0:T(8,128)}, u32[]{:S(2)}) copy-start(f32[128,1024]{1,0:T(8,128)} %get-tuple-element.54) | copy-start | bytes 1572868
  236.4 1.6 copy-start.3
  236.4 2.3 copy-start.4
  237.2 2.2 copy-start
